TPU v7x, 32 devices: a whole 2x2x4 slice. The times are simulated.
32 devices in a mesh: group: 4 (over y, x), seq: 8 (over z, core).
Axes of the slice: x: 2, y: 2, z: 4, core: 2. Of those that a mesh axis runs over, the one named last changes fastest.
Arguments:
- tokens: bfloat16 [32, 2048, 2048], P('group', 'seq'), may hold values from -6 to 6
- image_keys: bfloat16 [32, 256, 2048], P('group', 'seq'), may hold values from -256 to 256
- image_values: bfloat16 [32, 256, 2048], P('group', 'seq'), may hold values from -18 to 18
- text_len: int32 [32], replicated, may hold values from 1 to 2048
- image_len: int32 [32], replicated, may hold values from 1 to 256
- counts: int32 [6], replicated, may hold values from 1 to 4, as said below
- old_group: int32 [6], replicated, may hold values from 0 to 3, as said below
- new_group: int32 [6], replicated, may hold values from 0 to 3, as said below
- w_query: bfloat16 [2048, 2048], replicated, may hold values from -0.125 to 0.125
- w_out: bfloat16 [2048, 2048], replicated, may hold values from -0.125 to 0.125
Outputs:
- layer_out: bfloat16 [32, 2048, 2048], P('group', 'seq')
Inputs may be any that keep to these rules, and one draw needn't show every extreme that they name: `counts`: every task has at most 4 samples, and some task has exactly 4. `old_group`: each group is the old group of at most two tasks, and no two tasks share both their old group and their new group, so at most 4 samples go from one old group to one new group. `new_group`: each group is the new group of at most two tasks.
All inputs are finite; a program needn't handle non-finite values.
Results may differ from a plain program's by a relative error of at most 0.011.
Values may be sent and summed in bfloat16 or wider, within the bound.
A program may use at most 128 MiB of HBM per device.

v0:
```python
import jax
import jax.numpy as jnp
from jax import lax
from jax.sharding import PartitionSpec as P

HEAD_DIM = 128
HALF = 4
masked_score = -1e30
norm_eps = 1e-05


def layout(counts, old_group, new_group, group_count, slot_count):
    task_order = jnp.arange(counts.shape[0], dtype=jnp.int32)
    earlier = task_order[None, :] < task_order[:, None]
    same_old = old_group[None, :] == old_group[:, None]
    same_new = new_group[None, :] == new_group[:, None]
    old_start = jnp.sum(jnp.where(earlier & same_old, counts[None, :], 0), axis=1)
    new_start = jnp.sum(jnp.where(earlier & same_new, counts[None, :], 0), axis=1)
    target = jnp.arange(group_count * slot_count, dtype=jnp.int32)
    target_group = target // slot_count
    target_slot = target % slot_count
    matches = (
        (new_group[None, :] == target_group[:, None])
        & (target_slot[:, None] >= new_start[None, :])
        & (target_slot[:, None] < (new_start + counts)[None, :])
    )
    filled = jnp.any(matches, axis=1)
    offset = target_slot - jnp.sum(jnp.where(matches, new_start[None, :], 0), axis=1)
    source_group = jnp.sum(jnp.where(matches, old_group[None, :], 0), axis=1)
    source_slot = jnp.sum(jnp.where(matches, old_start[None, :], 0), axis=1) + offset
    return (filled, source_group, source_slot, offset, old_start)


def normalize(samples_rows):
    values = samples_rows.astype(jnp.float32)
    average = jnp.mean(values, axis=-1, keepdims=True)
    centred = values - average
    variance = jnp.mean(centred * centred, axis=-1, keepdims=True)
    return (centred * lax.rsqrt(variance + norm_eps)).astype(jnp.bfloat16)


def spread_rows(source_array, source_index, wanted):
    gathered = jnp.take(source_array, source_index, axis=0)
    return jnp.where(wanted[:, None, None], gathered, jnp.zeros((), source_array.dtype))


def regroup(joined, group_index, group_count, slot_count, tables, counts, old_group, new_group):
    filled, source_group, source_slot, offset, old_start = tables
    own_first = group_index * slot_count
    filled_here = lax.dynamic_slice_in_dim(filled, own_first, slot_count)
    from_group = lax.dynamic_slice_in_dim(source_group, own_first, slot_count)
    destinations = jnp.arange(group_count, dtype=jnp.int32)
    pairing = (old_group[None, :] == group_index) & (new_group[None, :] == destinations[:, None])
    pair_first = jnp.sum(jnp.where(pairing, old_start[None, :], 0), axis=1)
    pair_amount = jnp.sum(jnp.where(pairing, counts[None, :], 0), axis=1)
    position = jnp.arange(HALF, dtype=jnp.int32)
    sending = (position[None, :] < pair_amount[:, None]).reshape(-1)
    source_index = jnp.where(sending, (pair_first[:, None] + position[None, :]).reshape(-1), 0)
    outgoing = spread_rows(joined, source_index, sending)
    incoming = lax.all_to_all(outgoing, "group", split_axis=0, concat_axis=0, tiled=True)
    chosen = from_group * HALF + lax.dynamic_slice_in_dim(offset, own_first, slot_count)
    chosen = jnp.where(filled_here, chosen, 0)
    return spread_rows(incoming, chosen, filled_here)


def cross_layer(
    samples_rows, key_rows, value_rows, text_limit, key_limit, w_query, w_out, first_row
):
    slot_count, row_count, feature_count = samples_rows.shape
    head_count = w_query.shape[1] // HEAD_DIM
    normal = normalize(samples_rows).reshape(slot_count * row_count, feature_count)
    queries = (
        jnp.dot(normal, w_query, preferred_element_type=jnp.float32) * HEAD_DIM ** (-0.5)
    ).astype(jnp.bfloat16)
    queries = queries.reshape(slot_count, row_count, head_count, HEAD_DIM)
    running_max = jnp.full((slot_count, head_count, row_count), masked_score, jnp.float32)
    piece_keys = lax.all_gather(key_rows, "seq", axis=1, tiled=True)
    piece_values = lax.all_gather(value_rows, "seq", axis=1, tiled=True)
    key_count = piece_keys.shape[1]
    head_keys = piece_keys.reshape(slot_count, key_count, head_count, HEAD_DIM)
    head_values = piece_values.reshape(slot_count, key_count, head_count, HEAD_DIM)
    scores = jnp.einsum("sqhd,skhd->shqk", queries, head_keys, preferred_element_type=jnp.float32)
    position = jnp.arange(key_count, dtype=jnp.int32)
    allowed = (position[None, :] < key_limit[:, None])[:, None, None, :]
    scores = jnp.where(allowed, scores, masked_score)
    new_max = jnp.maximum(running_max, jnp.max(scores, axis=-1))
    probs = jnp.where(allowed, jnp.exp(scores - new_max[..., None]), 0.0)
    running_sum = jnp.sum(probs, axis=-1)
    weights = probs.astype(jnp.bfloat16)
    running_ctx = jnp.einsum(
        "shqk,skhd->shqd", weights, head_values, preferred_element_type=jnp.float32
    )
    running_max, running_sum, running_ctx = (new_max, running_sum, running_ctx)
    context = running_ctx / running_sum[..., None]
    context = (
        context.transpose(0, 2, 1, 3)
        .reshape(slot_count * row_count, head_count * HEAD_DIM)
        .astype(jnp.bfloat16)
    )
    projected = jnp.dot(context, w_out, preferred_element_type=jnp.float32).reshape(
        slot_count, row_count, feature_count
    )
    row_position = first_row + jnp.arange(row_count, dtype=jnp.int32)
    kept_rows = row_position[None, :] < text_limit[:, None]
    return jnp.where(kept_rows[..., None], projected, 0.0).astype(jnp.bfloat16)


def on_device(
    tokens,
    image_keys,
    image_values,
    text_len,
    image_len,
    counts,
    old_group,
    new_group,
    w_query,
    w_out,
):
    group_count = lax.axis_size("group")
    slot_count = tokens.shape[0]
    row_count = tokens.shape[1]
    group_index = lax.axis_index("group")
    first_row = lax.axis_index("seq") * row_count
    tables = layout(counts, old_group, new_group, group_count, slot_count)
    own_first = group_index * slot_count
    text_limit = lax.dynamic_slice_in_dim(text_len, own_first, slot_count)
    key_limit = lax.dynamic_slice_in_dim(image_len, own_first, slot_count)
    attended = cross_layer(
        tokens, image_keys, image_values, text_limit, key_limit, w_query, w_out, first_row
    )
    return regroup(
        attended, group_index, group_count, slot_count, tables, counts, old_group, new_group
    )


def solution(mesh):
    in_specs = (
        P("group", "seq", None),
        P("group", "seq", None),
        P("group", "seq", None),
        P(),
        P(),
        P(),
        P(),
        P(),
        P(),
        P(),
    )
    out_specs = P("group", "seq", None)
    return jax.shard_map(
        on_device, mesh=mesh, in_specs=in_specs, out_specs=out_specs, check_vma=False
    )
```

profile of v0, /device:TPU:0, one launch (start us, length us, event | category | flops | bytes accessed | tf_op | source)
XLA Modules:
  0.0 466.5 jit_solution(17421429270864026179)
XLA Ops:
  6.5 0.0 all-gather.3.cloned.1.call-start
  6.5 2.9 copy.28
  9.4 0.0 all-gather.3.cloned.1.call-update
  9.4 0.0 all-gather.5.cloned.1.call-start
  9.5 0.7 all-gather.5.cloned.1.call-update
  10.2 0.0 copy-start
  10.2 4.7 %convert_reduce_fusion = f32[8,256]{1,0:T(8,128)S(1)} fusion(bf16[8,256,2048]{2,1,0:T(8,128)(2,1)} %param.10), kind=kLoop, calls=%fused_computation.7 | loop fusion | flops 8386560 | bytes 8396800 | tf_op jit(solution)/shard_map/reduce_sum | solution.py:36
  14.9 1.1 copy-done
  16.0 2.4 fusion.4
  18.3 0.0 slice-start.1
  18.3 2.5 fusion.5
  20.9 0.0 slice-done
  20.9 0.1 slice-done.1
  21.0 19.4 %fusion.21 = bf16[256,8,16,128]{3,1,2,0:T(8,128)(2,1)} fusion(bf16[2048,2048]{1,0:T(8,128)(2,1)S(1)} %bitcast.27, bf16[2048,2048]{1,0:T(8,128)(2,1)S(1)} %bitcast.31), kind=kOutput, calls=%fused_computation.27 | convolution fusion | flops 17188257792 | bytes 25165824 | tf_op jit(solution)/shard_map/dot_general | solution.py:73
  40.3 0.0 copy-start.3
  40.3 9.8 %copy.38 = bf16[256,8,16,128]{3,2,1,0:T(8,128)(2,1)} copy(bf16[256,8,16,128]{3,1,2,0:T(8,128)(2,1)} %fusion.21) | data formatting | bytes 16777216
  50.1 0.0 copy-done.4
  50.1 0.1 dynamic_slice.19
  50.2 0.0 copy-done.5
  50.2 0.1 dynamic_slice.18
  50.3 0.0 copy-done.1
  50.3 0.0 copy-done.2
  50.3 0.0 copy-done.3
  50.3 0.2 select_reduce_fusion.4
  50.5 0.2 select_reduce_fusion.6
  50.7 0.1 iota_add_fusion
  50.8 0.1 select_n.139
  50.8 0.1 add.104
  50.9 0.1 iota_compare_fusion.3
  51.0 0.1 lt.144
  51.1 0.1 iota_compare_fusion
  51.2 0.1 broadcast_compare_fusion
  51.3 43.1 %all-gather.3.cloned.1.call-done = bf16[8,256,2048]{2,0,1:T(8,128)(2,1)} async-done(((bf16[8,32,2048]{2,0,1:T(8,128)(2,1)}), bf16[8,256,2048]{2,0,1:T(8,128)(2,1)}) %all-gather.3.cloned.1.call-update) | async-done | bytes 8388624 | tf_op jit(solution)/shard_map/all_gather | solution.py:77
  94.3 13.0 %copy.29 = bf16[8,256,2048]{1,2,0:T(8,128)(2,1)} copy(bf16[8,256,2048]{2,0,1:T(8,128)(2,1)} %all-gather.3.cloned.1.call-done) | data formatting | bytes 16777216 | tf_op jit(solution)/shard_map/all_gather | solution.py:77
  107.3 21.7 %select_reduce_fusion = (f32[8,16,256]{2,1,0:T(8,128)S(1)}, f32[8,16,256,256]{2,3,1,0:T(8,128)}) fusion(pred[8,256]{1,0:T(8,128)(4,1)S(1)} %iota_compare_fusion, bf16[8,256,16,128]{1,3,2,0:T(8,128)(2,1)} %bitcast.26, bf16[8,256,16,128]{3,2,1,0:T(8,128)(2,1)} %bitcast.25), kind=kOutput, calls=%fused_computation.3 | convolution fusion | flops 2164228096 | bytes 50464768 | tf_op jit(solution)/shard_map/sqhd,skhd->shqk/dot_general | solution.py:82
  129.1 14.7 %fusion = f32[8,16,256]{2,1,0:T(8,128)S(1)} fusion(f32[8,16,256,256]{2,3,1,0:T(8,128)} %get-tuple-element.18, f32[8,16,256]{2,1,0:T(8,128)S(1)} %broadcast_maximum_fusion, pred[8,256]{1,0:T(8,128)(4,1)S(1)} %iota_compare_fusion), kind=kLoop, calls=%fused_computation.4 | loop fusion | flops 33521664 | bytes 33818624 | tf_op jit(solution)/shard_map/reduce_sum | solution.py:88
  143.8 32.7 %all-gather.5.cloned.1.call-done = bf16[8,256,2048]{2,1,0:T(8,128)(2,1)} async-done(((bf16[8,32,2048]{2,1,0:T(8,128)(2,1)}), bf16[8,256,2048]{2,1,0:T(8,128)(2,1)}) %all-gather.5.cloned.1.call-update) | async-done | bytes 8388624 | tf_op jit(solution)/shard_map/all_gather | solution.py:78
  176.5 11.3 %copy.32 = bf16[8,256,2048]{1,2,0:T(8,128)(2,1)} copy(bf16[8,256,2048]{2,1,0:T(8,128)(2,1)} %all-gather.5.cloned.1.call-done) | data formatting | bytes 16777216 | tf_op jit(solution)/shard_map/all_gather | solution.py:78
  187.8 17.3 %fusion.8 = bf16[8,256,16,128]{1,3,2,0:T(8,128)(2,1)S(1)} fusion(f32[8,256,16]{1,2,0:T(8,128)S(1)} %bitcast.29, bf16[8,256,16,128]{1,3,2,0:T(8,128)(2,1)} %bitcast.28, f32[8,16,256,256]{2,3,1,0:T(8,128)} %get-tuple-element.18, f32[8,16,256]{2,1,0:T(8,128)S(1)} %broadcast_maximum_fusion, pred[8,256]{1,0:T(8,128)(4,1)S(1)} %iota_compare_fusion), kind=kOutput, calls=%fused_computation.14 | convolution fusion | flops 2189426688 | bytes 50595840 | tf_op jit(solution)/shard_map/shqk,skhd->shqd/dot_general | solution.py:90
  205.1 21.7 %select_convert_fusion = bf16[8,256,2048]{2,1,0:T(8,128)(2,1)} fusion(pred[8,256]{1,0:T(8,128)(4,1)S(1)} %broadcast_compare_fusion, bf16[8,256,2048]{1,2,0:T(8,128)(2,1)S(1)} %bitcast.32, bf16[2048,2048]{1,0:T(8,128)(2,1)} %param.19), kind=kOutput, calls=%fused_computation.16 | convolution fusion | flops 17188257792 | bytes 25167872 | tf_op jit(solution)/shard_map/dot_general | solution.py:100
  226.8 10.3 %gather_fusion = bf16[16,256,2048]{2,1,0:T(8,128)(2,1)} fusion(bf16[8,256,2048]{2,1,0:T(8,128)(2,1)} %select_convert_fusion, s32[1024]{0:T(1024)S(1)} %pad_clamp_fusion.1), kind=kCustom, calls=%fused_computation | custom fusion | bytes 33554496 | tf_op jit(solution)/shard_map/jit(_take)/gather | solution.py:43
  237.1 14.3 %select_select_fusion = bf16[16,256,2048]{2,1,0:T(8,128)(2,1)} fusion(bf16[16,256,2048]{2,1,0:T(8,128)(2,1)} %gather_fusion, pred[16]{0:T(512)(128)(4,1)S(1)} %compare_and_fusion.1, pred[16]{0:T(512)(128)(4,1)S(1)} %lt.144), kind=kLoop, calls=%fused_computation.15 | loop fusion | flops 16777216 | bytes 33554464 | tf_op jit(solution)/shard_map/jit(_where)/select_n | solution.py:44
  251.4 7.0 %all-to-all-start = ((bf16[16,256,2048]{2,1,0:T(8,128)(2,1)}), bf16[16,256,2048]{2,1,0:T(8,128)(2,1)}, u32[]{:S(2)}, u32[]{:S(2)}) async-start(bf16[16,256,2048]{2,1,0:T(8,128)(2,1)} %select_select_fusion), calls=%async_computation | async-start | bytes 33554432 | tf_op jit(solution)/shard_map/all_to_all | solution.py:60
  258.4 0.1 select_reduce_fusion.3
  258.5 0.1 compare_and_fusion.2
  258.6 182.7 %all-to-all-done = bf16[16,256,2048]{2,1,0:T(8,128)(2,1)} async-done(((bf16[16,256,2048]{2,1,0:T(8,128)(2,1)}), bf16[16,256,2048]{2,1,0:T(8,128)(2,1)}, u32[]{:S(2)}, u32[]{:S(2)}) %all-to-all-start) | async-done | bytes 16777248 | tf_op jit(solution)/shard_map/all_to_all | solution.py:60
  441.3 10.6 %gather_fusion.1 = bf16[8,256,2048]{2,1,0:T(8,128)(2,1)} fusion(bf16[16,256,2048]{2,1,0:T(8,128)(2,1)} %all-to-all-done, s32[1024]{0:T(1024)S(1)} %pad_clamp_fusion), kind=kCustom, calls=%fused_computation.1 | custom fusion | bytes 16777248 | tf_op jit(solution)/shard_map/jit(_take)/gather | solution.py:43
  451.9 7.7 %select_select_fusion.1 = bf16[8,256,2048]{2,1,0:T(8,128)(2,1)} fusion(bf16[8,256,2048]{2,1,0:T(8,128)(2,1)} %gather_fusion.1, pred[8]{0:T(512)(128)(4,1)S(1)} %get-tuple-element.11, pred[8]{0:T(512)(128)(4,1)S(1)} %get-tuple-element.13), kind=kLoop, calls=%fused_computation.26 | loop fusion | flops 8388608 | bytes 16777232 | tf_op jit(solution)/shard_map/jit(_where)/select_n | solution.py:44
  (19 shorter events, 0.1 us)
Async XLA Ops:
  6.5 87.8 %all-gather.3.cloned.1.call-start = ((), (), s32[]{:S(2)}) async-start(), calls=%async_computation.1 | async-start | bytes 9437184 | tf_op jit(solution)/shard_map/all_gather | solution.py:77
  9.4 167.1 %all-gather.5.cloned.1.call-start = ((), (), s32[]{:S(2)}) async-start(), calls=%async_computation.2 | async-start | bytes 9437184 | tf_op jit(solution)/shard_map/all_gather | solution.py:78
  10.2 5.8 %copy-start = (bf16[8,256,2048]{2,1,0:T(8,128)(2,1)S(1)}, bf16[8,256,2048]{2,1,0:T(8,128)(2,1)}, u32[]{:S(2)}) copy-start(bf16[8,256,2048]{2,1,0:T(8,128)(2,1)} %param.10) | copy-start | bytes 25165828
  16.0 4.9 %slice-start = ((s8[8388608]{0:T(1024)(128)(4,1)}), s8[4194304]{0:T(1024)(128)(4,1)S(1)}, s32[]{:S(2)}) async-start(s8[8388608]{0:T(1024)(128)(4,1)} %bitcast.30), calls=%async_computation.3 | async-start | bytes 8388608
  18.3 2.6 slice-start.1
  40.3 9.8 %copy-start.4 = (s32[32]{0:T(128)S(1)}, s32[32]{0:T(128)}, u32[]{:S(2)}) copy-start(s32[32]{0:T(128)} %param.14) | copy-start | bytes 388
  40.3 9.9 %copy-start.5 = (s32[32]{0:T(128)S(1)}, s32[32]{0:T(128)}, u32[]{:S(2)}) copy-start(s32[32]{0:T(128)} %param.13) | copy-start | bytes 388
  40.3 10.0 %copy-start.1 = (s32[6]{0:T(128)S(1)}, s32[6]{0:T(128)}, u32[]{:S(2)}) copy-start(s32[6]{0:T(128)} %param.17) | copy-start | bytes 76
  40.3 10.0 %copy-start.2 = (s32[6]{0:T(128)S(1)}, s32[6]{0:T(128)}, u32[]{:S(2)}) copy-start(s32[6]{0:T(128)} %param.16) | copy-start | bytes 76
  40.3 10.0 %copy-start.3 = (s32[6]{0:T(128)S(1)}, s32[6]{0:T(128)}, u32[]{:S(2)}) copy-start(s32[6]{0:T(128)} %param.15) | copy-start | bytes 76
  251.4 189.9 %all-to-all-start = ((bf16[16,256,2048]{2,1,0:T(8,128)(2,1)}), bf16[16,256,2048]{2,1,0:T(8,128)(2,1)}, u32[]{:S(2)}, u32[]{:S(2)}) async-start(bf16[16,256,2048]{2,1,0:T(8,128)(2,1)} %select_select_fusion), calls=%async_computation | async-start | bytes 33554432 | tf_op jit(solution)/shard_map/all_to_all | solution.py:60
Sparse Core Ops, SparseCore 0:
  9.6 84.7 all-gather.2
  95.9 80.5 all-gather.4
where the time goes:
time: 468 us; the launch traced here: 466 us
  waiting for transfers between devices  259 us (55%)
  matrix products  80.1 us (17%)
  local copies, waits for them, and re-layouts  59.4 us (13%)
  other arithmetic  47.2 us (10%)
  between operations  13.6 us (3%)
  starting transfers between devices  7 us (1%)
    all_to_all x1, waiting for transfers between devices, regroup(): lax.all_to_all(outgoing, 'group', split_axis=0, concat_axis=0, tiled=True)  183 us
    all_gather x1, waiting for transfers between devices, cross_layer(): piece_keys = lax.all_gather(key_rows, 'seq', axis=1, tiled=True)  43.1 us
    all_gather x1, waiting for transfers between devices, cross_layer(): piece_values = lax.all_gather(value_rows, 'seq', axis=1, tiled=True)  32.7 us
    select_n x2, other arithmetic, spread_rows(): jnp.where(wanted[:, None, None], gathered, jnp.zeros((), source_array.dty...  22 us
    dot_general x1, matrix products, cross_layer(): jnp.einsum('sqhd,skhd->shqk', queries, head_keys, preferred_element_type=...  21.7 us
    dot_general x1, matrix products, cross_layer(): jnp.dot(context, w_out, preferred_element_type=jnp.float32)  21.7 us
    gather x2, local copies, waits for them, and re-layouts, spread_rows(): gathered = jnp.take(source_array, source_index, axis=0)  20.9 us
    dot_general x1, matrix products, cross_layer(): jnp.dot(normal, w_query, preferred_element_type=jnp.float32)  19.4 us
  transfers between devices with their start and end apart: 3, of which 3 were waited for; matrix products, arithmetic and copies ran while one was open for 19% of the time, Pallas kernels for 0%

commit v1 on v0

--- a/solution.py
+++ b/solution.py
@@ -75,7 +75,18 @@
     queries = queries.reshape(slot_count, row_count, head_count, HEAD_DIM)
     running_max = jnp.full((slot_count, head_count, row_count), masked_score, jnp.float32)
     piece_keys = lax.all_gather(key_rows, "seq", axis=1, tiled=True)
-    piece_values = lax.all_gather(value_rows, "seq", axis=1, tiled=True)
+    n_dev_all = lax.axis_size("seq")
+    blocks_here = []
+    for j0 in range(1, n_dev_all):
+        blocks_here.append((j0 - 1, j0))
+    f_now = blocks_here + [(n_dev_all - 1, 0)]
+    finding = value_rows
+    series = [finding]
+    for _ in range(n_dev_all - 1):
+        finding = lax.ppermute(finding, "seq", f_now)
+        series += [finding]
+    local_next = jnp.concatenate([*reversed(series)], 1)
+    piece_values = jnp.roll(local_next, (lax.axis_index("seq") + 1) * finding.shape[1], 1)
     key_count = piece_keys.shape[1]
     head_keys = piece_keys.reshape(slot_count, key_count, head_count, HEAD_DIM)
     head_values = piece_values.reshape(slot_count, key_count, head_count, HEAD_DIM)

time: 468 us -> 553 us (1.18)
  waiting for transfers between devices: 259 us -> 301 us
  local copies, waits for them, and re-layouts: 59.4 us -> 93 us
    ppermute x0 -> x7, waiting for transfers between devices: none -> 126 us  [cross_layer(): finding = lax.ppermute(finding, 'seq', f_now)]
    all_gather x1, waiting for transfers between devices: 43.1 us -> 0.01 us  [cross_layer(): piece_keys = lax.all_gather(key_rows, 'seq', axis=1, tiled=True)]
    all_gather x1 -> x0, waiting for transfers between devices: 32.7 us -> none  [cross_layer(): piece_values = lax.all_gather(value_rows, 'seq', axis=1, tiled=True)]
    unnamed x18 -> x43, local copies, waits for them, and re-layouts: 13.8 us -> 38 us
    dynamic_slice x0 -> x2, local copies, waits for them, and re-layouts: none -> 19.9 us  [cross_layer(): jnp.roll(local_next, (lax.axis_index('seq') + 1) * finding.shape[1], 1)]
    all_gather x1 -> x0, local copies, waits for them, and re-layouts: 11.3 us -> none  [cross_layer(): piece_values = lax.all_gather(value_rows, 'seq', axis=1, tiled=True)]
    all_to_all x1, waiting for transfers between devices: 183 us -> 176 us  [regroup(): lax.all_to_all(outgoing, 'group', split_axis=0, concat_axis=0, tiled=True)]
  transfers between devices with their start and end apart: 3 -> 9, of which waited for: 3 -> 7; matrix products, arithmetic and copies ran while one was open for 19% -> 17% of each run, Pallas kernels for 0% -> 0%
where the time goes in v1:
time: 553 us; the launch traced here: 550 us
  waiting for transfers between devices  301 us (54%)
  local copies, waits for them, and re-layouts  93 us (17%)
  matrix products  83.6 us (15%)
  other arithmetic  51.1 us (9%)
  between operations  13.7 us (2%)
  starting transfers between devices  7.67 us (1%)
    all_to_all x1, waiting for transfers between devices, regroup(): lax.all_to_all(outgoing, 'group', split_axis=0, concat_axis=0, tiled=True)  176 us
    ppermute x7, waiting for transfers between devices, cross_layer(): finding = lax.ppermute(finding, 'seq', f_now)  126 us
    unnamed x43, local copies, waits for them, and re-layouts  38 us
    dot_general x1, matrix products, cross_layer(): jnp.dot(context, w_out, preferred_element_type=jnp.float32)  23.7 us
    select_n x2, other arithmetic, spread_rows(): jnp.where(wanted[:, None, None], gathered, jnp.zeros((), source_array.dty...  22 us
    dot_general x1, matrix products, cross_layer(): jnp.dot(normal, w_query, preferred_element_type=jnp.float32)  22 us
    dot_general x1, matrix products, cross_layer(): jnp.einsum('sqhd,skhd->shqk', queries, head_keys, preferred_element_type=...  21.7 us
    gather x2, local copies, waits for them, and re-layouts, spread_rows(): gathered = jnp.take(source_array, source_index, axis=0)  20.9 us
  transfers between devices with their start and end apart: 9, of which 7 were waited for; matrix products, arithmetic and copies ran while one was open for 17% of the time, Pallas kernels for 0%

profile of v1, /device:TPU:0, one launch (start us, length us, event | category | flops | bytes accessed | tf_op | source)
XLA Modules:
  0.0 550.3 jit_solution(11566205918324224974)
XLA Ops:
  6.5 0.5 collective-permute-start
  7.0 2.9 copy.28
  9.9 13.8 %collective-permute-done = bf16[8,32,2048]{2,1,0:T(8,128)(2,1)S(1)} collective-permute-done((bf16[8,32,2048]{2,1,0:T(8,128)(2,1)}, bf16[8,32,2048]{2,1,0:T(8,128)(2,1)S(1)}, u32[]{:S(2)}, u32[]{:S(2)}) %collective-permute-start) | collective-permute-done | bytes 1048608 | tf_op jit(solution)/shard_map/ppermute | solution.py:86
  23.8 38.6 %collective-permute-done.1 = bf16[8,32,2048]{2,1,0:T(8,128)(2,1)S(1)} collective-permute-done((bf16[8,32,2048]{2,1,0:T(8,128)(2,1)S(1)}, bf16[8,32,2048]{2,1,0:T(8,128)(2,1)S(1)}, u32[]{:S(2)}, u32[]{:S(2)}) %collective-permute-start.1) | collective-permute-done | bytes 1048608 | tf_op jit(solution)/shard_map/ppermute | solution.py:86
  62.4 38.6 %collective-permute-done.2 = bf16[8,32,2048]{2,1,0:T(8,128)(2,1)S(1)} collective-permute-done((bf16[8,32,2048]{2,1,0:T(8,128)(2,1)S(1)}, bf16[8,32,2048]{2,1,0:T(8,128)(2,1)S(1)}, u32[]{:S(2)}, u32[]{:S(2)}) %collective-permute-start.2) | collective-permute-done | bytes 1048608 | tf_op jit(solution)/shard_map/ppermute | solution.py:86
  101.0 4.9 convert_reduce_fusion
  106.0 5.9 %fusion.4 = f32[8,256]{1,0:T(8,128)S(1)} fusion(bf16[8,256,2048]{2,1,0:T(8,128)(2,1)} %param.10, f32[8,256]{1,0:T(8,128)S(1)} %broadcast_multiply_fusion), kind=kLoop, calls=%fused_computation.10 | loop fusion | flops 16775168 | bytes 8404992 | tf_op jit(solution)/shard_map/reduce_sum | solution.py:38
  111.9 14.8 %collective-permute-done.3 = bf16[8,32,2048]{2,1,0:T(8,128)(2,1)S(1)} collective-permute-done((bf16[8,32,2048]{2,1,0:T(8,128)(2,1)S(1)}, bf16[8,32,2048]{2,1,0:T(8,128)(2,1)S(1)}, u32[]{:S(2)}, u32[]{:S(2)}) %collective-permute-start.3) | collective-permute-done | bytes 1048608 | tf_op jit(solution)/shard_map/ppermute | solution.py:86
  126.7 2.4 fusion.5
  129.1 13.7 %collective-permute-done.4 = bf16[8,32,2048]{2,1,0:T(8,128)(2,1)} collective-permute-done((bf16[8,32,2048]{2,1,0:T(8,128)(2,1)S(1)}, bf16[8,32,2048]{2,1,0:T(8,128)(2,1)}, u32[]{:S(2)}, u32[]{:S(2)}) %collective-permute-start.4) | collective-permute-done | bytes 1048608 | tf_op jit(solution)/shard_map/ppermute | solution.py:86
  142.8 22.0 %fusion.21 = bf16[256,8,16,128]{3,1,2,0:T(8,128)(2,1)} fusion(bf16[2048,2048]{1,0:T(8,128)(2,1)S(1)} %bitcast.29, bf16[2048,2048]{1,0:T(8,128)(2,1)} %param.18), kind=kOutput, calls=%fused_computation.27 | convolution fusion | flops 17188257792 | bytes 25165824 | tf_op jit(solution)/shard_map/dot_general | solution.py:73
  164.8 0.2 select_reduce_fusion.4
  165.1 0.1 select_reduce_fusion.6
  165.4 0.2 collective-permute-start.6
  165.6 9.7 %copy.38 = bf16[256,8,16,128]{3,2,1,0:T(8,128)(2,1)} copy(bf16[256,8,16,128]{3,1,2,0:T(8,128)(2,1)} %fusion.21) | data formatting | bytes 16777216
  175.7 0.1 lt.156
  175.9 6.0 %collective-permute-done.6 = bf16[8,32,2048]{2,1,0:T(8,128)(2,1)} collective-permute-done((bf16[8,32,2048]{2,1,0:T(8,128)(2,1)}, bf16[8,32,2048]{2,1,0:T(8,128)(2,1)}, u32[]{:S(2)}, u32[]{:S(2)}) %collective-permute-start.6) | collective-permute-done | bytes 1048608 | tf_op jit(solution)/shard_map/ppermute | solution.py:86
  181.9 2.3 constant_dynamic-update-slice_fusion.15
  184.2 2.3 constant_dynamic-update-slice_fusion.14
  186.5 2.3 constant_dynamic-update-slice_fusion.13
  188.7 2.3 constant_dynamic-update-slice_fusion.12
  191.0 2.3 constant_dynamic-update-slice_fusion.11
  193.3 1.0 constant_dynamic-update-slice_fusion.10
  194.3 1.0 constant_dynamic-update-slice_fusion.9
  195.3 1.0 constant_dynamic-update-slice_fusion.8
  196.4 2.3 constant_dynamic-update-slice_fusion.7
  198.7 2.3 constant_dynamic-update-slice_fusion.6
  200.9 2.3 constant_dynamic-update-slice_fusion.5
  203.2 1.0 constant_dynamic-update-slice_fusion.4
  204.2 1.0 constant_dynamic-update-slice_fusion.3
  205.2 1.0 constant_dynamic-update-slice_fusion.2
  206.2 1.0 constant_dynamic-update-slice_fusion.1
  207.3 1.0 constant_dynamic-update-slice_fusion
  208.3 8.4 %constant_dynamic-slice_fusion = bf16[8,256,2048]{2,1,0:T(8,128)(2,1)} fusion(bf16[8,512,2048]{2,1,0:T(8,128)(2,1)} %constant_dynamic-update-slice_fusion, s32[]{:T(128)S(6)} %select_n.150), kind=kLoop, calls=%fused_computation.79 | loop fusion | bytes 16777220 | tf_op jit(solution)/shard_map/jit(_roll_dynamic)/dynamic_slice | solution.py:89
  216.7 11.4 %copy.32 = bf16[8,256,2048]{1,2,0:T(8,128)(2,1)} copy(bf16[8,256,2048]{2,1,0:T(8,128)(2,1)} %constant_dynamic-slice_fusion) | data formatting | bytes 16777216 | tf_op jit(solution)/shard_map/jit(_roll_dynamic)/dynamic_slice | solution.py:89
  228.1 12.8 %copy.29 = bf16[8,256,2048]{1,2,0:T(8,128)(2,1)} copy(bf16[8,256,2048]{2,0,1:T(8,128)(2,1)} %all-gather.2.cloned.1.call-done) | data formatting | bytes 16777216 | tf_op jit(solution)/shard_map/all_gather | solution.py:77
  241.0 21.7 %select_reduce_fusion = (f32[8,16,256]{2,1,0:T(8,128)S(1)}, f32[8,16,256,256]{2,3,1,0:T(8,128)}) fusion(pred[8,256]{1,0:T(8,128)(4,1)S(1)} %iota_compare_fusion, bf16[8,256,16,128]{1,3,2,0:T(8,128)(2,1)} %bitcast.28, bf16[8,256,16,128]{3,2,1,0:T(8,128)(2,1)} %bitcast.27), kind=kOutput, calls=%fused_computation.3 | convolution fusion | flops 2164228096 | bytes 50464768 | tf_op jit(solution)/shard_map/sqhd,skhd->shqk/dot_general | solution.py:93
  262.7 15.0 %fusion = f32[8,16,256]{2,1,0:T(8,128)S(1)} fusion(f32[8,16,256,256]{2,3,1,0:T(8,128)} %get-tuple-element.18, f32[8,16,256]{2,1,0:T(8,128)S(1)} %broadcast_maximum_fusion, pred[8,256]{1,0:T(8,128)(4,1)S(1)} %iota_compare_fusion), kind=kLoop, calls=%fused_computation.4 | loop fusion | flops 33521664 | bytes 33818624 | tf_op jit(solution)/shard_map/reduce_sum | solution.py:99
  277.7 16.3 %fusion.8 = bf16[8,256,16,128]{1,3,2,0:T(8,128)(2,1)} fusion(f32[8,256,16]{1,2,0:T(8,128)S(1)} %bitcast.31, bf16[8,256,16,128]{1,3,2,0:T(8,128)(2,1)S(1)} %bitcast.30, f32[8,16,256,256]{2,3,1,0:T(8,128)} %get-tuple-element.18, f32[8,16,256]{2,1,0:T(8,128)S(1)} %broadcast_maximum_fusion, pred[8,256]{1,0:T(8,128)(4,1)S(1)} %iota_compare_fusion), kind=kOutput, calls=%fused_computation.14 | convolution fusion | flops 2189426688 | bytes 50595840 | tf_op jit(solution)/shard_map/shqk,skhd->shqd/dot_general | solution.py:101
  294.0 23.7 %select_convert_fusion = bf16[8,256,2048]{2,1,0:T(8,128)(2,1)} fusion(pred[8,256]{1,0:T(8,128)(4,1)S(1)} %broadcast_compare_fusion, bf16[8,256,2048]{1,2,0:T(8,128)(2,1)} %bitcast.32, bf16[2048,2048]{1,0:T(8,128)(2,1)} %param.19), kind=kOutput, calls=%fused_computation.16 | convolution fusion | flops 17188257792 | bytes 25167872 | tf_op jit(solution)/shard_map/dot_general | solution.py:111
  317.7 10.3 %gather_fusion = bf16[16,256,2048]{2,1,0:T(8,128)(2,1)} fusion(bf16[8,256,2048]{2,1,0:T(8,128)(2,1)} %select_convert_fusion, s32[1024]{0:T(1024)S(1)} %pad_clamp_fusion.1), kind=kCustom, calls=%fused_computation | custom fusion | bytes 33554496 | tf_op jit(solution)/shard_map/jit(_take)/gather | solution.py:43
  328.0 14.3 %select_select_fusion = bf16[16,256,2048]{2,1,0:T(8,128)(2,1)} fusion(bf16[16,256,2048]{2,1,0:T(8,128)(2,1)} %gather_fusion, pred[16]{0:T(512)(128)(4,1)S(1)} %compare_and_fusion.1, pred[16]{0:T(512)(128)(4,1)S(1)} %lt.156), kind=kLoop, calls=%fused_computation.15 | loop fusion | flops 16777216 | bytes 33554464 | tf_op jit(solution)/shard_map/jit(_where)/select_n | solution.py:44
  342.3 7.0 %all-to-all-start = ((bf16[16,256,2048]{2,1,0:T(8,128)(2,1)}), bf16[16,256,2048]{2,1,0:T(8,128)(2,1)}, u32[]{:S(2)}, u32[]{:S(2)}) async-start(bf16[16,256,2048]{2,1,0:T(8,128)(2,1)} %select_select_fusion), calls=%async_computation | async-start | bytes 33554432 | tf_op jit(solution)/shard_map/all_to_all | solution.py:60
  349.3 0.1 select_reduce_fusion.3
  349.4 0.1 compare_and_fusion.2
  349.5 175.6 %all-to-all-done = bf16[16,256,2048]{2,1,0:T(8,128)(2,1)} async-done(((bf16[16,256,2048]{2,1,0:T(8,128)(2,1)}), bf16[16,256,2048]{2,1,0:T(8,128)(2,1)}, u32[]{:S(2)}, u32[]{:S(2)}) %all-to-all-start) | async-done | bytes 16777248 | tf_op jit(solution)/shard_map/all_to_all | solution.py:60
  525.1 10.6 %gather_fusion.1 = bf16[8,256,2048]{2,1,0:T(8,128)(2,1)} fusion(bf16[16,256,2048]{2,1,0:T(8,128)(2,1)} %all-to-all-done, s32[1024]{0:T(1024)S(1)} %pad_clamp_fusion), kind=kCustom, calls=%fused_computation.1 | custom fusion | bytes 16777248 | tf_op jit(solution)/shard_map/jit(_take)/gather | solution.py:43
  535.7 7.7 %select_select_fusion.1 = bf16[8,256,2048]{2,1,0:T(8,128)(2,1)} fusion(bf16[8,256,2048]{2,1,0:T(8,128)(2,1)} %gather_fusion.1, pred[8]{0:T(512)(128)(4,1)S(1)} %get-tuple-element.11, pred[8]{0:T(512)(128)(4,1)S(1)} %get-tuple-element.13), kind=kLoop, calls=%fused_computation.26 | loop fusion | flops 8388608 | bytes 16777232 | tf_op jit(solution)/shard_map/jit(_where)/select_n | solution.py:44
  (57 shorter events, 0.8 us)
Async XLA Ops:
  6.5 221.6 %all-gather.2.cloned.1.call-start = ((), (), s32[]{:S(2)}) async-start(), calls=%async_computation.1 | async-start | bytes 9437184 | tf_op jit(solution)/shard_map/all_gather | solution.py:77
  6.5 17.2 %collective-permute-start = (bf16[8,32,2048]{2,1,0:T(8,128)(2,1)}, bf16[8,32,2048]{2,1,0:T(8,128)(2,1)S(1)}, u32[]{:S(2)}, u32[]{:S(2)}) collective-permute-start(bf16[8,32,2048]{2,1,0:T(8,128)(2,1)} %param.12), channel_id=1, source_target_pairs={{0,1},{1,2},{2,3},{3,4},{4,5},{5,6},{6,7},{7,0},{8,9},{9,10},{10,1... | collective-permute-start | bytes 3145736 | tf_op jit(solution)/shard_map/ppermute | solution.py:86
  9.9 116.8 %slice-start = ((s8[8388608]{0:T(1024)(128)(4,1)}), s8[4194304]{0:T(1024)(128)(4,1)S(1)}, s32[]{:S(2)}) async-start(s8[8388608]{0:T(1024)(128)(4,1)} %bitcast.25), calls=%async_computation.2 | async-start | bytes 8388608
  23.8 38.6 %collective-permute-start.1 = (bf16[8,32,2048]{2,1,0:T(8,128)(2,1)S(1)}, bf16[8,32,2048]{2,1,0:T(8,128)(2,1)S(1)}, u32[]{:S(2)}, u32[]{:S(2)}) collective-permute-start(bf16[8,32,2048]{2,1,0:T(8,128)(2,1)S(1)} %collective-permute-done), channel_id=1, source_target_pairs={{0,1},{1,2},{2,3},{3,4},{4,5},{5,6},{6,7},{7,0},{8,9},{9,10},{10,1... | collective-permute-start | bytes 3145736 | tf_op jit(solution)/shard_map/ppermute | solution.py:86
  62.4 38.6 %collective-permute-start.2 = (bf16[8,32,2048]{2,1,0:T(8,128)(2,1)S(1)}, bf16[8,32,2048]{2,1,0:T(8,128)(2,1)S(1)}, u32[]{:S(2)}, u32[]{:S(2)}) collective-permute-start(bf16[8,32,2048]{2,1,0:T(8,128)(2,1)S(1)} %collective-permute-done.1), channel_id=1, source_target_pairs={{0,1},{1,2},{2,3},{3,4},{4,5},{5,6},{6,7},{7,0},{8,9},{9,10},{10,1... | collective-permute-start | bytes 3145736 | tf_op jit(solution)/shard_map/ppermute | solution.py:86
  101.0 28.1 %copy-start.2 = (bf16[8,32,2048]{2,1,0:T(8,128)(2,1)}, bf16[8,32,2048]{2,1,0:T(8,128)(2,1)S(1)}, u32[]{:S(2)}) copy-start(bf16[8,32,2048]{2,1,0:T(8,128)(2,1)S(1)} %collective-permute-done.2) | copy-start | bytes 3145732
  101.0 25.7 %collective-permute-start.3 = (bf16[8,32,2048]{2,1,0:T(8,128)(2,1)S(1)}, bf16[8,32,2048]{2,1,0:T(8,128)(2,1)S(1)}, u32[]{:S(2)}, u32[]{:S(2)}) collective-permute-start(bf16[8,32,2048]{2,1,0:T(8,128)(2,1)S(1)} %collective-permute-done.2), channel_id=1, source_target_pairs={{0,1},{1,2},{2,3},{3,4},{4,5},{5,6},{6,7},{7,0},{8,9},{9,10},{10,1... | collective-permute-start | bytes 3145736 | tf_op jit(solution)/shard_map/ppermute | solution.py:86
  105.9 20.8 %slice-start.1 = ((s8[8388608]{0:T(1024)(128)(4,1)}), s8[4194304]{0:T(1024)(128)(4,1)S(1)}, s32[]{:S(2)}) async-start(s8[8388608]{0:T(1024)(128)(4,1)} %bitcast.25), calls=%async_computation.3 | async-start | bytes 8388608
  126.7 38.1 %copy-start.4 = (bf16[8,32,2048]{2,1,0:T(8,128)(2,1)}, bf16[8,32,2048]{2,1,0:T(8,128)(2,1)S(1)}, u32[]{:S(2)}) copy-start(bf16[8,32,2048]{2,1,0:T(8,128)(2,1)S(1)} %collective-permute-done.3) | copy-start | bytes 3145732
  126.7 16.1 %collective-permute-start.4 = (bf16[8,32,2048]{2,1,0:T(8,128)(2,1)S(1)}, bf16[8,32,2048]{2,1,0:T(8,128)(2,1)}, u32[]{:S(2)}, u32[]{:S(2)}) collective-permute-start(bf16[8,32,2048]{2,1,0:T(8,128)(2,1)S(1)} %collective-permute-done.3), channel_id=1, source_target_pairs={{0,1},{1,2},{2,3},{3,4},{4,5},{5,6},{6,7},{7,0},{8,9},{9,10},{10,1... | collective-permute-start | bytes 3145736 | tf_op jit(solution)/shard_map/ppermute | solution.py:86
  142.8 22.6 %collective-permute-start.5 = (bf16[8,32,2048]{2,1,0:T(8,128)(2,1)}, bf16[8,32,2048]{2,1,0:T(8,128)(2,1)}, u32[]{:S(2)}, u32[]{:S(2)}) collective-permute-start(bf16[8,32,2048]{2,1,0:T(8,128)(2,1)} %collective-permute-done.4), channel_id=1, source_target_pairs={{0,1},{1,2},{2,3},{3,4},{4,5},{5,6},{6,7},{7,0},{8,9},{9,10},{10,1... | collective-permute-start | bytes 3145736 | tf_op jit(solution)/shard_map/ppermute | solution.py:86
  142.8 22.0 %copy-start.6 = (s32[6]{0:T(128)S(1)}, s32[6]{0:T(128)}, u32[]{:S(2)}) copy-start(s32[6]{0:T(128)} %param.17) | copy-start | bytes 76
  142.8 22.0 %copy-start.7 = (s32[6]{0:T(128)S(1)}, s32[6]{0:T(128)}, u32[]{:S(2)}) copy-start(s32[6]{0:T(128)} %param.16) | copy-start | bytes 76
  142.8 22.0 %copy-start.8 = (s32[6]{0:T(128)S(1)}, s32[6]{0:T(128)}, u32[]{:S(2)}) copy-start(s32[6]{0:T(128)} %param.15) | copy-start | bytes 76
  164.8 10.6 %copy-start.9 = (s32[32]{0:T(128)S(1)}, s32[32]{0:T(128)}, u32[]{:S(2)}) copy-start(s32[32]{0:T(128)} %param.14) | copy-start | bytes 388
  164.8 10.6 %copy-start.10 = (s32[32]{0:T(128)S(1)}, s32[32]{0:T(128)}, u32[]{:S(2)}) copy-start(s32[32]{0:T(128)} %param.13) | copy-start | bytes 388
  164.8 30.6 %copy-start.1 = (bf16[8,32,2048]{2,1,0:T(8,128)(2,1)S(1)}, bf16[8,32,2048]{2,1,0:T(8,128)(2,1)}, u32[]{:S(2)}) copy-start(bf16[8,32,2048]{2,1,0:T(8,128)(2,1)} %param.12) | copy-start | bytes 3145732
  165.4 16.5 %collective-permute-start.6 = (bf16[8,32,2048]{2,1,0:T(8,128)(2,1)}, bf16[8,32,2048]{2,1,0:T(8,128)(2,1)}, u32[]{:S(2)}, u32[]{:S(2)}) collective-permute-start(bf16[8,32,2048]{2,1,0:T(8,128)(2,1)} %collective-permute-done.5), channel_id=1, source_target_pairs={{0,1},{1,2},{2,3},{3,4},{4,5},{5,6},{6,7},{7,0},{8,9},{9,10},{10,1... | collective-permute-start | bytes 3145736 | tf_op jit(solution)/shard_map/ppermute | solution.py:86
  175.8 27.5 %copy-start.5 = (bf16[8,32,2048]{2,1,0:T(8,128)(2,1)S(1)}, bf16[8,32,2048]{2,1,0:T(8,128)(2,1)}, u32[]{:S(2)}) copy-start(bf16[8,32,2048]{2,1,0:T(8,128)(2,1)} %copy-done.4) | copy-start | bytes 3145732
  175.8 28.5 %copy-start.3 = (bf16[8,32,2048]{2,1,0:T(8,128)(2,1)S(1)}, bf16[8,32,2048]{2,1,0:T(8,128)(2,1)}, u32[]{:S(2)}) copy-start(bf16[8,32,2048]{2,1,0:T(8,128)(2,1)} %copy-done.2) | copy-start | bytes 3145732
  262.7 15.0 %copy-start = (bf16[8,256,2048]{1,2,0:T(8,128)(2,1)S(1)}, bf16[8,256,2048]{1,2,0:T(8,128)(2,1)}, u32[]{:S(2)}) copy-start(bf16[8,256,2048]{1,2,0:T(8,128)(2,1)} %copy.32) | copy-start | bytes 25165828
  342.3 182.8 %all-to-all-start = ((bf16[16,256,2048]{2,1,0:T(8,128)(2,1)}), bf16[16,256,2048]{2,1,0:T(8,128)(2,1)}, u32[]{:S(2)}, u32[]{:S(2)}) async-start(bf16[16,256,2048]{2,1,0:T(8,128)(2,1)} %select_select_fusion), calls=%async_computation | async-start | bytes 33554432 | tf_op jit(solution)/shard_map/all_to_all | solution.py:60
Sparse Core Ops, SparseCore 0:
  10.0 111.1 all-gather.1
